TPU v7x, 256 devices: a whole 4x4x8 slice. The times are simulated.
256 devices in a mesh: section: 8 (over z), expert: 2 (over core), tensor: 16 (over y, x).
Axes of the slice: x: 4, y: 4, z: 8, core: 2. Of those that a mesh axis runs over, the one named last changes fastest.
Arguments:
- tokens: bfloat16 [8192, 6144], P(('section', 'expert'), 'tensor'), may hold values from -6 to 6
- norm_gain: float32 [4, 6144], P(None, 'tensor'), may hold values from 0.5 to 1.5
- router: float32 [4, 6144, 8], P(None, 'tensor'), may hold values from -0.078125 to 0.078125
- w_gate: bfloat16 [8, 2, 6144, 4096], P('section', 'expert', None, 'tensor'), may hold values from -0.078125 to 0.078125
- w_up: bfloat16 [8, 2, 6144, 4096], P('section', 'expert', None, 'tensor'), may hold values from -0.078125 to 0.078125
- w_down: bfloat16 [8, 2, 4096, 6144], P('section', 'expert', 'tensor'), may hold values from -0.0625 to 0.0625
- expert_ids: int32 [2, 8192, 2], P(None, ('section', 'expert')), may hold values from 0 to 7, all different within a row
- lengths: int32 [8, 8], P(None, 'expert'), may hold values from 32 to 128
Outputs:
- encoded: bfloat16 [8192, 6144], P(('section', 'expert'), 'tensor')
All inputs are finite; a program needn't handle non-finite values.
Results may differ from a plain program's by a relative error of at most 0.006.
Values may be sent and summed in bfloat16 or wider, within the bound.
A program may use at most 64 MiB of HBM per device.

v0:
```python
import jax
import jax.numpy as jnp
from jax import lax
from jax.sharding import PartitionSpec as P

D = 6144
E = 8
EXP_WIN = 2
SEQ_LEN = 128
STEPS = 2
CAP = 64


norm_eps = 1e-05


def swapped(x, axis, bit):
    return lax.ppermute(x, axis, [(i, i ^ 1 << bit) for i in range(lax.axis_size(axis))])


def from_behind(x, axis, by):
    peers = lax.axis_size(axis)
    return lax.ppermute(x, axis, [(i, (i + by) % peers) for i in range(peers)])


def route_tables(choice_ids, seq_lens, gate_logits):
    token_count = choice_ids.shape[0]
    expert_range = jnp.arange(E, dtype=jnp.int32)
    match_ids = choice_ids[:, :, None] == expert_range[None, None, :]
    one_hot = match_ids.astype(jnp.float32)
    picked = jnp.sum(gate_logits[:, None, :] * one_hot, axis=2)
    first_weight = jax.nn.sigmoid(picked[:, 0] - picked[:, 1])
    second_weight = jax.nn.sigmoid(picked[:, 1] - picked[:, 0])
    dense_gates = (
        first_weight[:, None] * one_hot[:, 0, :] + second_weight[:, None] * one_hot[:, 1, :]
    )
    dense_gates = dense_gates[:, :EXP_WIN]
    positions = jnp.arange(token_count, dtype=jnp.int32)
    live_rows = positions % SEQ_LEN < jnp.repeat(seq_lens, SEQ_LEN, total_repeat_length=token_count)
    named = jnp.any(match_ids, axis=1)[:, :EXP_WIN] & live_rows[:, None]
    named_int = named.astype(jnp.int32)
    earlier = jnp.cumsum(named_int, axis=0) - named_int
    slot_range = jnp.arange(CAP, dtype=jnp.int32)
    placed = named[None, :, :] & (earlier[None, :, :] == slot_range[:, None, None])
    route_table = jnp.transpose(placed.astype(jnp.float32), (2, 0, 1))
    return (route_table, route_table * jnp.transpose(dense_gates)[:, None, :])


def moe_layer(
    layer_rows, gain_row, router_matrix, gate_w, up_w, down_w, choice_ids, seq_lens, expert_count
):
    as_float = layer_rows.astype(jnp.float32)
    scaled = as_float * gain_row[None, :]
    part_logits = jnp.dot(scaled, router_matrix, precision=lax.Precision.HIGHEST)
    square_sum, logit_sum = lax.psum((jnp.sum(as_float * as_float, axis=1), part_logits), "tensor")
    inv_rms = lax.rsqrt(square_sum / D + norm_eps)
    normed = (scaled * inv_rms[:, None]).astype(jnp.bfloat16)
    gate_logits = inv_rms[:, None] * logit_sum
    route_table, weighted = route_tables(choice_ids, seq_lens, gate_logits)
    fsplit_count = expert_count // EXP_WIN
    table_narrow = route_table.astype(jnp.bfloat16)
    feature_count = normed.shape[1]
    picked_rows = jnp.einsum(
        "ecr,rd->ecd", table_narrow, normed, preferred_element_type=jnp.float32
    ).astype(jnp.bfloat16)
    widened = jnp.broadcast_to(picked_rows[:, None], (EXP_WIN, fsplit_count, CAP, feature_count))
    arrived = lax.all_to_all(
        widened.reshape(expert_count, CAP, feature_count),
        "expert",
        split_axis=0,
        concat_axis=1,
        tiled=True,
    )
    partner = swapped(arrived, "section", 0)
    held_rows = jnp.concatenate([arrived, partner], axis=1)
    feature_piece = lax.all_gather(held_rows, "tensor", axis=2, tiled=True)
    col_count = feature_piece.shape[2]
    gate_part = lax.slice_in_dim(gate_w, 0, col_count, axis=1)
    up_part = lax.slice_in_dim(up_w, 0, col_count, axis=1)
    gate_more = jnp.einsum(
        "snd,sdf->snf", feature_piece, gate_part, preferred_element_type=jnp.float32
    )
    up_more = jnp.einsum("snd,sdf->snf", feature_piece, up_part, preferred_element_type=jnp.float32)
    hidden = (jax.nn.silu(gate_more) * up_more).astype(jnp.bfloat16)
    partial_out = jnp.einsum("snf,sfd->snd", hidden, down_w, preferred_element_type=jnp.float32)
    summed = lax.psum_scatter(
        partial_out.astype(jnp.bfloat16), "tensor", scatter_dimension=2, tiled=True
    )
    own_count = summed.shape[1] // 2
    own_part = summed[:, :own_count]
    other_part = summed[:, own_count:]
    from_partner = swapped(other_part, "section", 0)
    slab_out = (own_part.astype(jnp.float32) + from_partner.astype(jnp.float32)).astype(
        jnp.bfloat16
    )
    returned = lax.all_to_all(slab_out, "expert", split_axis=1, concat_axis=0, tiled=True)
    half_width = returned.shape[2]
    per_expert = jnp.sum(
        returned.reshape(EXP_WIN, fsplit_count, CAP, half_width).astype(jnp.float32), axis=1
    )
    mixture = jnp.einsum("ecr,ecd->rd", weighted, per_expert, precision=lax.Precision.HIGHEST)
    return (as_float + mixture).astype(jnp.bfloat16)


def on_device(tokens, norm_gain, router, w_gate, w_up, w_down, expert_ids, lengths):
    section_count = lax.axis_size("section")
    section_place = lax.axis_index("section")
    expert_count = lax.axis_size("expert")
    layer_place = section_place // 2
    gain_row = lax.dynamic_index_in_dim(norm_gain, layer_place, 0, keepdims=False)
    router_matrix = lax.dynamic_index_in_dim(router, layer_place, 0, keepdims=False)
    current = tokens
    for step_index in range(STEPS):
        micro_batch = (section_place - 2 * step_index) % section_count
        seq_lens = lax.dynamic_index_in_dim(lengths, micro_batch, 0, keepdims=False)
        current = moe_layer(
            current,
            gain_row,
            router_matrix,
            w_gate[0],
            w_up[0],
            w_down[0],
            expert_ids[step_index],
            seq_lens,
            expert_count,
        )
        if step_index + 1 < STEPS:
            current = from_behind(current, "section", 2)
    return current


def solution(mesh):
    in_specs = (
        P(("section", "expert"), "tensor"),
        P(None, "tensor"),
        P(None, "tensor", None),
        P("section", "expert", None, "tensor"),
        P("section", "expert", None, "tensor"),
        P("section", "expert", "tensor", None),
        P(None, ("section", "expert"), None),
        P(None, "expert"),
    )
    out_specs = P(("section", "expert"), "tensor")
    return jax.shard_map(
        on_device, mesh=mesh, in_specs=in_specs, out_specs=out_specs, check_vma=False
    )
```

profile of v0, /device:TPU:1, one launch (start us, length us, event | category | flops | bytes accessed | tf_op | source)
XLA Modules:
  0.0 600.9 jit_solution(5741067348918299058)
XLA Ops:
  9.3 1.8 fusion.21
  11.1 61.2 %all-reduce.1 = (f32[512]{0:T(512)S(1)}, f32[512,8]{0,1:T(8,128)}) all-reduce(f32[512]{0:T(512)S(1)} %fusion.26, f32[512,8]{0,1:T(8,128)S(1)} %fusion.21), channel_id=1, replica_groups=mesh['section'=8,'expert'=2,'tensor'=16] {'tensor'}, use_global_device_ids=true, to_apply=%region_4.6 | all-reduce | flops 4608 | bytes 36864 | tf_op jit(solution)/shard_map/psum | solution.py:55
  74.6 2.5 select_compare_fusion.1
  80.2 18.3 %all_to_all.42 = bf16[2,64,384]{2,1,0:T(8,128)(2,1)S(1)} all-to-all(bf16[2,64,384]{2,1,0:T(8,128)(2,1)S(1)} %convolution_convert_fusion.3), channel_id=1, replica_groups=mesh['section'=8,'expert'=2,'tensor'=16] {'expert'}, dimensions={0} | all-to-all | bytes 196608 | tf_op jit(solution)/shard_map/all_to_all | solution.py:67
  100.2 2.7 collective-permute-done
  103.7 53.6 %all-gather.3.cloned.1.call-done = bf16[1,256,6144]{2,1,0:T(8,128)(2,1)} async-done(((bf16[1,256,384]{2,1,0:T(8,128)(2,1)}), bf16[1,256,6144]{2,1,0:T(8,128)(2,1)}) %all-gather.3.cloned.1.call-update) | async-done | bytes 3145744 | tf_op jit(solution)/shard_map/all_gather | solution.py:76
  157.3 3.8 fusion.9
  161.1 8.0 %fusion = bf16[1,256,6144]{2,1,0:T(8,128)(2,1)} fusion(bf16[1,1,256,6144]{3,2,1,0:T(8,128)(2,1)S(1)} %copy-done, f32[256,256]{1,0:T(8,128)S(1)} %fusion.9, bf16[1,1,6144,256]{3,2,1,0:T(8,128)(2,1)} %param.17, bf16[1,256,6144]{2,1,0:T(8,128)(2,1)} %all-gather.3.cloned.1.call-done), kind=kOutput, calls=%fused_computation.2 | convolution fusion | flops 1612578816 | bytes 12845056 | tf_op jit(solution)/shard_map/snf,sfd->snd/dot_general | solution.py:85
  169.1 13.9 %copy.13 = bf16[1,256,6144]{1,0,2:T(2,128)(2,1)} copy(bf16[1,256,6144]{2,1,0:T(8,128)(2,1)} %fusion) | data formatting | bytes 6291456
  183.1 5.0 copy.34
  188.2 2.6 select_compare_fusion
  194.1 75.0 %reduce-scatter.7.cloned.1.call-done = bf16[384,256]{1,0:T(8,128)(2,1)} async-done(((bf16[6144,256]{1,0:T(8,128)(2,1)}), bf16[384,256]{1,0:T(8,128)(2,1)}) %reduce-scatter.7.cloned.1.call-update) | async-done | bytes 196624
  271.4 1.7 copy.22
  279.4 2.7 reduce.13
  283.6 8.5 %all_to_all.43 = bf16[2,2,12288]{2,1,0:T(2,128)(2,1)} all-to-all(bf16[2,2,12288]{2,1,0:T(2,128)(2,1)} %reshape.217), channel_id=1, replica_groups=mesh['section'=8,'expert'=2,'tensor'=16] {'expert'}, dimensions={0} | all-to-all | bytes 196608 | tf_op jit(solution)/shard_map/all_to_all | solution.py:96
  296.0 2.3 collective-permute-start.2
  299.7 14.5 %collective-permute-done.2 = bf16[512,384]{1,0:T(8,128)(2,1)S(1)} collective-permute-done((bf16[512,384]{1,0:T(8,128)(2,1)S(1)}, bf16[512,384]{1,0:T(8,128)(2,1)S(1)}, u32[]{:S(2)}, u32[]{:S(2)}) %collective-permute-start.2) | collective-permute-done | bytes 393248 | tf_op jit(solution)/shard_map/ppermute | solution.py:23
  316.4 58.0 %all-reduce = (f32[512]{0:T(512)}, f32[512,8]{0,1:T(8,128)}) all-reduce(f32[512]{0:T(512)} %fusion.27, f32[512,8]{0,1:T(8,128)S(1)} %fusion.23), channel_id=1, replica_groups=mesh['section'=8,'expert'=2,'tensor'=16] {'tensor'}, use_global_device_ids=true, to_apply=%region_12.14 | all-reduce | flops 4608 | bytes 36864 | tf_op jit(solution)/shard_map/psum | solution.py:55
  376.1 18.4 %all_to_all.44 = bf16[2,64,384]{2,1,0:T(8,128)(2,1)S(1)} all-to-all(bf16[2,64,384]{2,1,0:T(8,128)(2,1)S(1)} %convolution_convert_fusion.2), channel_id=1, replica_groups=mesh['section'=8,'expert'=2,'tensor'=16] {'expert'}, dimensions={0} | all-to-all | bytes 196608 | tf_op jit(solution)/shard_map/all_to_all | solution.py:67
  394.6 4.4 collective-permute-start.3
  398.9 2.8 collective-permute-done.3
  402.5 52.4 %all-gather.5.cloned.1.call-done = bf16[1,256,6144]{2,1,0:T(8,128)(2,1)} async-done(((bf16[1,256,384]{2,1,0:T(8,128)(2,1)}), bf16[1,256,6144]{2,1,0:T(8,128)(2,1)}) %all-gather.5.cloned.1.call-update) | async-done | bytes 3145744 | tf_op jit(solution)/shard_map/all_gather | solution.py:76
  454.9 4.5 fusion.2
  459.4 8.0 %fusion.1 = bf16[1,256,6144]{2,1,0:T(8,128)(2,1)} fusion(bf16[1,1,256,6144]{3,2,1,0:T(8,128)(2,1)S(1)} %copy-done, f32[256,256]{1,0:T(8,128)} %fusion.2, bf16[1,256,6144]{2,1,0:T(8,128)(2,1)} %all-gather.5.cloned.1.call-done, bf16[1,1,6144,256]{3,2,1,0:T(8,128)(2,1)} %param.17), kind=kOutput, calls=%fused_computation.3 | convolution fusion | flops 1612578816 | bytes 12845056 | tf_op jit(solution)/shard_map/snf,sfd->snd/dot_general | solution.py:85
  467.4 13.9 %copy.15 = bf16[1,256,6144]{1,0,2:T(2,128)(2,1)} copy(bf16[1,256,6144]{2,1,0:T(8,128)(2,1)} %fusion.1) | data formatting | bytes 6291456
  481.4 5.0 copy.33
  488.5 78.9 %reduce-scatter.9.cloned.1.call-done = bf16[384,256]{1,0:T(8,128)(2,1)} async-done(((bf16[6144,256]{1,0:T(8,128)(2,1)}), bf16[384,256]{1,0:T(8,128)(2,1)}) %reduce-scatter.9.cloned.1.call-update) | async-done | bytes 196624
  569.7 1.7 copy.24
  573.3 1.7 copy.23
  576.9 2.7 reduce.14
  581.2 8.7 %all_to_all.45 = bf16[2,2,12288]{2,1,0:T(2,128)(2,1)} all-to-all(bf16[2,2,12288]{2,1,0:T(2,128)(2,1)} %reshape.219), channel_id=1, replica_groups=mesh['section'=8,'expert'=2,'tensor'=16] {'expert'}, dimensions={0} | all-to-all | bytes 196608 | tf_op jit(solution)/shard_map/all_to_all | solution.py:96
  592.4 2.0 fusion.18
  (90 shorter events, 46.3 us)
Async XLA Ops:
  6.5 154.6 %copy-start = (bf16[1,1,256,6144]{3,2,1,0:T(8,128)(2,1)S(1)}, bf16[1,1,256,6144]{3,2,1,0:T(8,128)(2,1)}, u32[]{:S(2)}) copy-start(bf16[1,1,256,6144]{3,2,1,0:T(8,128)(2,1)} %param.19) | copy-start | bytes 9437188
  6.5 150.7 %all-gather.3.cloned.1.call-start = ((), (), s32[]{:S(2)}) async-start(), calls=%async_computation.6 | async-start | bytes 3342336 | tf_op jit(solution)/shard_map/all_gather | solution.py:76
  8.5 95.1 %copy-start.2 = (s32[512,2]{0,1:T(2,128)}, s32[512,2]{0,1:T(2,128)S(1)}, u32[]{:S(2)}) copy-start(s32[512,2]{0,1:T(2,128)S(1)} %get-tuple-element.40) | copy-start | bytes 12292
  9.3 94.4 %copy-start.4 = (f32[384]{0:T(512)}, f32[384]{0:T(512)S(1)}, u32[]{:S(2)}) copy-start(f32[384]{0:T(512)S(1)} %dynamic-slice_reduce_fusion.2) | copy-start | bytes 4612
  72.3 31.3 %copy-start.5 = (f32[512]{0:T(512)}, f32[512]{0:T(512)S(1)}, u32[]{:S(2)}) copy-start(f32[512]{0:T(512)S(1)} %add_rsqrt_fusion.1) | copy-start | bytes 6148
  77.2 26.5 %copy-start.10 = (pred[2,512]{1,0:T(4,128)(4,1)}, pred[2,512]{1,0:T(4,128)(4,1)S(1)}, u32[]{:S(2)}) copy-start(pred[2,512]{1,0:T(4,128)(4,1)S(1)} %get-tuple-element.44) | copy-start | bytes 3076
  78.3 0.6 copy-start.8
  98.5 4.3 collective-permute-start
  103.6 165.5 %reduce-scatter.7.cloned.1.call-start = ((), (), s32[]{:S(2)}) async-start(), calls=%async_computation.8 | async-start | bytes 3342336
  188.1 106.7 %copy-start.1 = (bf16[512,384]{1,0:T(8,128)(2,1)S(1)}, bf16[512,384]{1,0:T(8,128)(2,1)}, u32[]{:S(2)}) copy-start(bf16[512,384]{1,0:T(8,128)(2,1)} %param.14) | copy-start | bytes 1179652
  188.1 266.8 %all-gather.5.cloned.1.call-start = ((), (), s32[]{:S(2)}) async-start(), calls=%async_computation.7 | async-start | bytes 3342336 | tf_op jit(solution)/shard_map/all_gather | solution.py:76
  190.8 0.6 copy-start.6
  192.0 107.1 %copy-start.7 = (pred[512]{0:T(512)(128)(4,1)S(1)}, pred[512]{0:T(512)(128)(4,1)}, u32[]{:S(2)}) copy-start(pred[512]{0:T(512)(128)(4,1)} %copy-done.6) | copy-start | bytes 1540
  273.1 3.9 collective-permute-start.1
  296.0 18.2 %collective-permute-start.2 = (bf16[512,384]{1,0:T(8,128)(2,1)S(1)}, bf16[512,384]{1,0:T(8,128)(2,1)S(1)}, u32[]{:S(2)}, u32[]{:S(2)}) collective-permute-start(bf16[512,384]{1,0:T(8,128)(2,1)S(1)} %fusion.19), channel_id=1, source_target_pairs={{0,64},{32,96},{64,128},{96,160},{128,192},{160,224},{192,0},{224,... | collective-permute-start | bytes 1179656 | tf_op jit(solution)/shard_map/ppermute | solution.py:23
  394.6 7.2 %collective-permute-start.3 = (bf16[1,128,384]{2,1,0:T(8,128)(2,1)S(1)}, bf16[1,128,384]{2,1,0:T(8,128)(2,1)S(1)}, u32[]{:S(2)}, u32[]{:S(2)}) collective-permute-start(bf16[1,128,384]{2,1,0:T(8,128)(2,1)S(1)} %bitcast.192), channel_id=1, source_target_pairs={{0,32},{32,0},{64,96},{96,64},{128,160},{160,128},{192,224},{224,1... | collective-permute-start | bytes 294920 | tf_op jit(solution)/shard_map/ppermute | solution.py:18
  402.5 164.9 %reduce-scatter.9.cloned.1.call-start = ((), (), s32[]{:S(2)}) async-start(), calls=%async_computation.9 | async-start | bytes 3342336
  486.4 2.1 copy-start.3
  486.4 106.1 %copy-start.9 = (s32[2,512]{1,0:T(2,128)S(1)}, s32[2,512]{1,0:T(2,128)}, u32[]{:S(2)}) copy-start(s32[2,512]{1,0:T(2,128)} %fusion.83) | copy-start | bytes 12292
  571.3 3.8 collective-permute-start.4
Sparse Core Ops, SparseCore 0:
  103.7 53.5 all-gather.2
  188.2 80.8 reduce-scatter.6
  402.6 52.2 all-gather.4
  486.5 80.8 reduce-scatter.8
where the time goes:
time: 603 us; the launch traced here: 601 us
  waiting for transfers between devices  280 us (46%)
  blocking collectives  173 us (29%)
  local copies, waits for them, and re-layouts  65.9 us (11%)
  matrix products  33.2 us (6%)
  other arithmetic  24.3 us (4%)
  between operations  13.3 us (2%)
  starting transfers between devices  11 us (2%)
    unnamed x6, waiting for transfers between devices  154 us
    psum x2, blocking collectives, moe_layer(): lax.psum((jnp.sum(as_float * as_float, axis=1), part_logits), 'tensor')  119 us
    all_gather x2, waiting for transfers between devices, moe_layer(): feature_piece = lax.all_gather(held_rows, 'tensor', axis=2, tiled=True)  106 us
    unnamed x39, local copies, waits for them, and re-layouts  56.4 us
    all_to_all x2, blocking collectives, moe_layer(): lax.all_to_all(widened.reshape(expert_count, CAP, feature_count), 'expert...  36.8 us
    all_to_all x2, blocking collectives, moe_layer(): lax.all_to_all(slab_out, 'expert', split_axis=1, concat_axis=0, tiled=True)  17.2 us
    dot_general x2, matrix products, moe_layer(): jnp.einsum('snf,sfd->snd', hidden, down_w, preferred_element_type=jnp.flo...  16 us
    ppermute x1, waiting for transfers between devices, from_behind(): return lax.ppermute(x, axis, [(i, (i + by) % peers) for i in range(peers)])  14.5 us
  transfers between devices with their start and end apart: 9, of which 8 were waited for; matrix products, arithmetic and copies ran while one was open for 2% of the time, Pallas kernels for 0%

commit v1 on v0

v1 whole, which is shorter than its diff:
```python
import functools

import jax
import jax.numpy as jnp
from jax import lax
from jax.experimental import pallas as pl
from jax.experimental.pallas import tpu as pltpu
from jax.sharding import PartitionSpec as P

D = 6144
E = 8
SEQ_LEN = 128
STEPS = 2
CAP = 64
NORM_EPS = 1e-05
N_SEC = 8
TOK = 512
FEAT = 384
HID = 256

MESH = pl.DeviceIdType.MESH
HIGHEST = lax.Precision.HIGHEST
F32 = jnp.float32
BF16 = jnp.bfloat16
NT = (((1,), (1,)), ((), ()))
TN = (((0,), (0,)), ((), ()))


def gray(i):
    return i + (i // 2) * (1 - 2 * (i % 2))


def kernel(
    x_ref, gain_ref, router_ref, gate_hbm, up_hbm, down_hbm, ids_ref, lens_ref, out_ref,
    w_in, w_down, tri, xc, xn, one_hot, slots, slots_in, rows_out,
    ag, acc, hid, pb, passed, landed, mixed, ring, final, back,
    stat, stat_x, stat_y, scales, scales_in,
    w_sem, ag_sem, ag_send, rs_sem, rs_send, ex_send, stat_sem, stat_send,
    scale_sem, scale_send, back_sem, back_send, tok_sem, tok_send,
):
    sec = lax.axis_index("section")
    core = lax.axis_index("expert")
    t = lax.axis_index("tensor")
    py, px = t // 4, t % 4
    par = sec % 2
    mate = sec + 1 - 2 * par
    ahead = (sec + 2) % N_SEC
    mate_ahead = (mate + 2) % N_SEC
    behind = (sec + 6) % N_SEC
    mate_behind = (mate + 6) % N_SEC
    other = 1 - core
    layer = sec // 2

    def at(dx, dy):
        return ((py + dy + 4) % 4) * 4 + (px + dx + 4) % 4

    def shard(s, cf, cq):
        return at(cf, cq) if s == 0 else at(cq, cf)

    def near(s, role, d):
        off = (d, 0) if role == s else (0, d)
        return (sec, core, at(*off))

    w_copies = [
        pltpu.make_async_copy(gate_hbm, w_in.at[:, :, pl.ds(0, HID)], w_sem.at[0]),
        pltpu.make_async_copy(up_hbm, w_in.at[:, :, pl.ds(HID, HID)], w_sem.at[1]),
        pltpu.make_async_copy(down_hbm, w_down, w_sem.at[2]),
    ]
    for c in w_copies:
        c.start()

    barrier = pltpu.get_barrier_semaphore()
    peers = [(sec, core, at(d, 0)) for d in (1, 2, 3)] + [(sec, core, at(0, d)) for d in (1, 2, 3)]
    peers.append((sec, other, t))
    for there in (mate, ahead, mate_ahead, behind, mate_behind):
        peers += [(there, 0, t), (there, 1, t)]
    for peer in peers:
        pl.semaphore_signal(barrier, inc=1, device_id=peer, device_id_type=MESH)

    xc[...] = x_ref[...]
    tri[...] = (
        lax.broadcasted_iota(jnp.int32, (TOK, TOK), 0) < lax.broadcasted_iota(jnp.int32, (TOK, TOK), 1)
    ).astype(F32).astype(BF16)
    pl.semaphore_wait(barrier, len(peers))

    def remote(src, dst, send, recv, dev):
        return pltpu.make_async_remote_copy(
            src_ref=src, dst_ref=dst, send_sem=send, recv_sem=recv, device_id=dev, device_id_type=MESH
        )

    def step(st, carry):
        first = ids_ref[st, pl.ds(0, 1), :]
        second = ids_ref[st, pl.ds(1, 1), :]
        batch = (sec + 8 - 2 * st) % N_SEC
        lane = lax.broadcasted_iota(jnp.int32, (1, SEQ_LEN), 1)
        live = jnp.concatenate(
            [(lane < lens_ref[batch, q]).astype(jnp.int32) for q in range(TOK // SEQ_LEN)], axis=1
        )
        row_id = lax.broadcasted_iota(jnp.int32, (8, TOK), 0)
        named = (
            ((first == row_id) | (second == row_id)).astype(F32)
            * live.astype(F32)
            * (row_id < 2).astype(F32)
        )
        earlier = jnp.dot(named.astype(BF16), tri[...], preferred_element_type=F32)
        slot = jnp.where((named > 0.5) & (earlier < CAP - 0.5), earlier, -1.0)
        slots[st] = slot
        spot = lax.broadcasted_iota(jnp.int32, (CAP, TOK), 0).astype(F32)
        for e in range(2):
            one_hot[pl.ds(e * CAP, CAP), :] = (slot[e : e + 1, :] == spot).astype(F32).astype(BF16)
        picks = one_hot[...]
        rows = jnp.dot(picks, xc[...], preferred_element_type=F32)
        scaled = rows * gain_ref[pl.ds(layer, 1), :]
        rows_out[st] = scaled.astype(BF16).reshape(2, CAP, FEAT)

        pltpu.make_async_copy(rows_out.at[st, core], ag.at[st, t, core, 0], ag_sem.at[st, t, core, 0]).start()
        remote(
            rows_out.at[st, other], ag.at[st, t, core, 0], ex_send.at[st], ag_sem.at[st, t, core, 0],
            (sec, other, t),
        ).start()
        for e in range(2):
            remote(
                rows_out.at[st, e], ag.at[st, t, core, 1], ex_send.at[st], ag_sem.at[st, t, core, 1],
                (mate, e, t),
            ).start()

        sub = lax.broadcasted_iota(jnp.int32, (8, 2 * CAP), 0)
        half = lax.broadcasted_iota(jnp.int32, (8, 2 * CAP), 1) // CAP
        squares = lax.dot_general(jnp.ones((8, FEAT), F32), rows * rows, NT, precision=HIGHEST, preferred_element_type=F32)
        logits = lax.dot_general(router_ref[layer], scaled, NT, precision=HIGHEST, preferred_element_type=F32)
        chosen = []
        for e in range(2):
            rest = jnp.where(first == e, second, first)
            chosen.append(
                lax.dot_general(
                    (rest == row_id).astype(F32).astype(BF16), picks, NT, preferred_element_type=F32
                )
            )
        rival = jnp.where(half == 0, chosen[0], chosen[1])
        gap = jnp.sum(logits * ((sub == half).astype(F32) - rival), axis=0, keepdims=True)
        stat[st, 0] = jnp.where(sub == 0, squares, jnp.where(sub == 1, gap, 0.0))
        for d in (1, 2, 3):
            remote(
                stat.at[st, 0], stat_x.at[st, d - 1], stat_send.at[st, d - 1], stat_sem.at[st, d - 1],
                (sec, core, at(d, 0)),
            ).start()

        @pl.when(st == 0)
        def _():
            remote(slots.at[0], slots_in, tok_send.at[0], tok_sem.at[0], (ahead, core, t)).start()
            remote(x_ref, xn, tok_send.at[1], tok_sem.at[1], (ahead, core, t)).start()

        def unit_send(s, sg, which, role, d):
            remote(
                ag.at[st, which, s, sg], ag.at[st, which, s, sg], ag_send.at[st],
                ag_sem.at[st, which, s, sg], near(s, role, d),
            ).start()

        def unit_wait(s, sg, which):
            remote(
                ag.at[st, which, s, sg], ag.at[st, which, s, sg], ag_send.at[st],
                ag_sem.at[st, which, s, sg], (sec, other, t),
            ).wait_recv()

        def across(s, sg, which):
            for d in (1, -1):
                unit_send(s, sg, which, 1, d)

        def own(sg):
            for s in range(2):
                unit_wait(s, sg, t)
            for s in range(2):
                for d in (1, -1):
                    unit_send(s, sg, t, 0, d)
            for s in range(2):
                across(s, sg, t)

        own(0)
        total = stat[st, 0]
        for d in (1, 2, 3):
            remote(
                stat.at[st, 0], stat_x.at[st, d - 1], stat_send.at[st, d - 1], stat_sem.at[st, d - 1],
                (sec, core, at(d, 0)),
            ).wait_recv()
            total = total + stat_x[st, d - 1]
        stat[st, 1] = total
        for d in (1, 2, 3):
            remote(
                stat.at[st, 1], stat_y.at[st, d - 1], stat_send.at[st, d + 2], stat_sem.at[st, d + 2],
                (sec, core, at(0, d)),
            ).start()
        own(1)
        for s in range(2):
            left, right = shard(s, -1, 0), shard(s, 1, 0)
            unit_wait(s, 0, left)
            unit_send(s, 0, left, 0, 1)
            across(s, 0, left)
            unit_wait(s, 0, right)
            across(s, 0, right)
        for d in (1, 2, 3):
            remote(
                stat.at[st, 1], stat_y.at[st, d - 1], stat_send.at[st, d + 2], stat_sem.at[st, d + 2],
                (sec, core, at(0, d)),
            ).wait_recv()
            total = total + stat_y[st, d - 1]
        inv = lax.rsqrt(total[0:1, :] / D + NORM_EPS)
        share = jax.nn.sigmoid(inv * total[1:2, :])
        scale = jnp.where(sub == 0, inv, jnp.where(sub == 1, share, 0.0))
        scales[st, 0] = scale
        scales[st, 1] = pltpu.roll(scale, CAP, 1)
        pltpu.make_async_copy(scales.at[st, core], scales_in.at[st, 0, core], scale_sem.at[st, 0, core]).start()
        remote(
            scales.at[st, other], scales_in.at[st, 0, core], scale_send.at[st], scale_sem.at[st, 0, core],
            (sec, other, t),
        ).start()
        for e in range(2):
            remote(
                scales.at[st, e], scales_in.at[st, 1, core], scale_send.at[st], scale_sem.at[st, 1, core],
                (mate, e, t),
            ).start()
        for s in range(2):
            left, right = shard(s, -1, 0), shard(s, 1, 0)
            unit_wait(s, 1, right)
            unit_send(s, 1, right, 0, -1)
            across(s, 1, right)
            unit_wait(s, 1, left)
            across(s, 1, left)
        for s in range(2):
            far = shard(s, 2, 0)
            for sg in range(2):
                unit_wait(s, sg, far)
                across(s, sg, far)

        acc[...] = jnp.zeros_like(acc)

        @pl.when(st == 0)
        def _():
            w_copies[0].wait()
            w_copies[1].wait()

        def multiply(s, which):
            acc[s] += jnp.dot(
                ag[st, which, s].reshape(2 * CAP, FEAT), w_in[which], preferred_element_type=F32
            )

        def column(i, carry):
            c = gray(i)
            for s in range(2):
                left, right = shard(s, c, -1), shard(s, c, 1)
                unit_wait(s, 0, left)
                unit_send(s, 0, left, 1, 1)
                unit_wait(s, 1, right)
                unit_send(s, 1, right, 1, -1)
            for s in range(2):
                multiply(s, shard(s, c, 0))
            for s in range(2):
                left, right = shard(s, c, -1), shard(s, c, 1)
                unit_wait(s, 1, left)
                multiply(s, left)
                unit_wait(s, 0, right)
                multiply(s, right)
            return carry

        lax.fori_loop(0, 4, column, 0)

        def far_column(i, carry):
            c = gray(i)
            for s in range(2):
                far = shard(s, c, 2)
                unit_wait(s, 0, far)
                unit_wait(s, 1, far)
                multiply(s, far)
            return carry

        lax.fori_loop(0, 4, far_column, 0)

        for sg in range(2):
            for s in range(2):
                remote(
                    scales.at[st, 0], scales_in.at[st, sg, s], scale_send.at[st], scale_sem.at[st, sg, s],
                    (sec, other, t),
                ).wait_recv()
                turned = scales_in[st, sg, s].T
                inv_col = turned[:CAP, 0:1]
                share_col = turned[:CAP, 1:2]
                part = acc[s, pl.ds(sg * CAP, CAP), :]
                gate = part[:, :HID] * inv_col
                up = part[:, HID:] * inv_col
                hidden = gate / (1.0 + jnp.exp(-gate)) * up * share_col
                hid[s, pl.ds(sg * CAP, CAP), :] = hidden.astype(BF16)

        @pl.when(st == 0)
        def _():
            w_copies[2].wait()

        def ring_send(s, k, m, src, dst, role, d):
            remote(src, dst, rs_send.at[st], rs_sem.at[st, s, k, m], near(s, role, d)).start()

        def ring_wait(s, k, m, dst):
            remote(dst, dst, rs_send.at[st], rs_sem.at[st, s, k, m], (sec, other, t)).wait_recv()

        def send_far(s, k, src, role):
            ring_send(s, k, 0, src.at[0], passed.at[st, s, k, 0], role, 1)
            ring_send(s, k, 1, src.at[1], passed.at[st, s, k, 1], role, -1)

        def send_right(s, k, src, role):
            ring_send(s, k, 2, src.at[1], landed.at[st, s, k, 0, 1], role, 1)

        def send_left(s, k, src, role):
            ring_send(s, k, 3, src.at[0], landed.at[st, s, k, 1, 0], role, -1)

        def pass_on(s, k, right_src, left_src, role):
            ring_wait(s, k, 0, passed.at[st, s, k, 0])
            mixed[st, s, k, 0] = (right_src[0].astype(F32) + passed[st, s, k, 0].astype(F32)).astype(BF16)
            ring_send(s, k, 4, mixed.at[st, s, k, 0], landed.at[st, s, k, 0, 0], role, 1)
            ring_wait(s, k, 1, passed.at[st, s, k, 1])
            mixed[st, s, k, 1] = (left_src[1].astype(F32) + passed[st, s, k, 1].astype(F32)).astype(BF16)
            ring_send(s, k, 5, mixed.at[st, s, k, 1], landed.at[st, s, k, 1, 1], role, -1)

        def finish(s, k, mine):
            ring_wait(s, k, 2, landed.at[st, s, k, 0, 1])
            ring_wait(s, k, 3, landed.at[st, s, k, 1, 0])
            ring_wait(s, k, 4, landed.at[st, s, k, 0, 0])
            ring_wait(s, k, 5, landed.at[st, s, k, 1, 1])
            return (
                mine[...].astype(F32)
                + landed[st, s, k, 0].astype(F32)
                + landed[st, s, k, 1].astype(F32)
            ).astype(BF16)

        def part_of(s, c, j, k, cj):
            which = shard(s, c, cj)
            cols = pl.ds(pl.multiple_of(which * FEAT, 128), FEAT)
            value = jnp.dot(hid[s], w_down[:, cols], preferred_element_type=F32)
            pb[st, s, k, j] = value.astype(BF16).reshape(2, CAP, FEAT)
            return pb.at[st, s, k, j]

        def wave(i, carry):
            @pl.when(i < 4)
            def _():
                c = gray(3 - i)
                for s in range(2):
                    send_far(s, i, part_of(s, c, 0, i, 2), 1)
                for s in range(2):
                    send_right(s, i, part_of(s, c, 1, i, 1), 1)
                    send_left(s, i, part_of(s, c, 2, i, -1), 1)
                for s in range(2):
                    part_of(s, c, 3, i, 0)

            @pl.when((i >= 1) & (i < 5))
            def _():
                k = i - 1
                for s in range(2):
                    pass_on(s, k, pb.at[st, s, k, 1], pb.at[st, s, k, 2], 1)

            @pl.when(i >= 2)
            def _():
                k = i - 2
                for s in range(2):
                    ring[st, s, k] = finish(s, k, pb.at[st, s, k, 3])

                @pl.when(k == 0)
                def _():
                    for s in range(2):
                        send_far(s, 4, ring.at[st, s, 0], 0)

                @pl.when(k == 1)
                def _():
                    for s in range(2):
                        send_left(s, 4, ring.at[st, s, 1], 0)

                @pl.when(k == 2)
                def _():
                    for s in range(2):
                        send_right(s, 4, ring.at[st, s, 2], 0)
                        pass_on(s, 4, ring.at[st, s, 2], ring.at[st, s, 1], 0)

            return carry

        lax.fori_loop(0, 6, wave, 0)
        for s in range(2):
            final[st, s] = finish(s, 4, ring.at[st, s, 3])

        def back_wait():
            for e in range(2):
                for b in range(2):
                    remote(
                        final.at[st, 0, 0], back.at[st, e, b], back_send.at[st], back_sem.at[st, e, b],
                        (sec, other, t),
                    ).wait_recv()

        def combined(base, table):
            slab = (back[st, :, 0].astype(F32) + back[st, :, 1].astype(F32)).astype(BF16)
            mix = lax.dot_general(
                table, slab.reshape(2 * CAP, FEAT), TN, preferred_element_type=F32
            )
            return (base.astype(F32) + mix).astype(BF16)

        @pl.when(st == 0)
        def _():
            for s in range(2):
                for sg, there in ((0, ahead), (1, mate_ahead)):
                    remote(
                        final.at[0, s, sg], back.at[0, core, par], back_send.at[0], back_sem.at[0, core, par],
                        (there, s, t),
                    ).start()
            remote(slots.at[0], slots_in, tok_send.at[0], tok_sem.at[0], (ahead, core, t)).wait_recv()
            remote(x_ref, xn, tok_send.at[1], tok_sem.at[1], (ahead, core, t)).wait_recv()
            for e in range(2):
                one_hot[pl.ds(e * CAP, CAP), :] = (
                    slots_in[e : e + 1, :] == spot
                ).astype(F32).astype(BF16)
            table = one_hot[...]
            back_wait()
            xc[...] = combined(xn[...], table)

        @pl.when(st == 1)
        def _():
            pltpu.make_async_copy(final.at[1, core, 0], back.at[1, core, par], back_sem.at[1, core, par]).start()
            remote(
                final.at[1, other, 0], back.at[1, core, par], back_send.at[1], back_sem.at[1, core, par],
                (sec, other, t),
            ).start()
            for s in range(2):
                remote(
                    final.at[1, s, 1], back.at[1, core, par], back_send.at[1], back_sem.at[1, core, par],
                    (mate, s, t),
                ).start()
            back_wait()
            out_ref[...] = combined(xc[...], one_hot[...])

        sixty = ag.at[st, pl.ds(0, 15)]
        remote(sixty, sixty, ag_send.at[st], ag_sem.at[st, 0, 0, 0], (sec, other, t)).wait_send()
        remote(sixty, sixty, rs_send.at[st], ag_sem.at[st, 0, 0, 0], (sec, other, t)).wait_send()
        three = ag.at[st, 0, 0]
        one = ag.at[st, 0, 0, 0]
        for sem in (ex_send,):
            remote(three, three, sem.at[st], ag_sem.at[st, 0, 0, 0], (sec, other, t)).wait_send()
            remote(one, one, sem.at[st], ag_sem.at[st, 0, 0, 0], (sec, other, t)).wait_send()
        tiles = stat_x.at[st]
        remote(tiles, tiles, scale_send.at[st], ag_sem.at[st, 0, 0, 0], (sec, other, t)).wait_send()
        for d in range(6):
            remote(stat.at[st, 0], stat.at[st, 0], stat_send.at[st, d], stat_sem.at[st, d], (sec, other, t)).wait_send()

        @pl.when(st == 0)
        def _():
            four = ag.at[st, 0]
            remote(four, four, back_send.at[0], ag_sem.at[st, 0, 0, 0], (sec, other, t)).wait_send()
            remote(slots.at[0], slots_in, tok_send.at[0], tok_sem.at[0], (ahead, core, t)).wait_send()
            remote(x_ref, xn, tok_send.at[1], tok_sem.at[1], (ahead, core, t)).wait_send()

        @pl.when(st == 1)
        def _():
            remote(three, three, back_send.at[1], ag_sem.at[st, 0, 0, 0], (sec, other, t)).wait_send()
            remote(one, one, back_send.at[1], ag_sem.at[st, 0, 0, 0], (sec, other, t)).wait_send()

        return carry

    lax.fori_loop(0, STEPS, step, 0)


def on_device(tokens, norm_gain, router, w_gate, w_up, w_down, expert_ids, lengths):
    vmem = pl.BlockSpec(memory_space=pltpu.VMEM)
    anywhere = pl.BlockSpec(memory_space=pl.ANY)
    unit = (CAP, FEAT)
    tile = (8, 2 * CAP)
    dma = pltpu.SemaphoreType.DMA
    return pl.pallas_call(
        kernel,
        out_shape=jax.ShapeDtypeStruct((TOK, FEAT), BF16),
        in_specs=[vmem, vmem, vmem, anywhere, anywhere, anywhere, vmem, pl.BlockSpec(memory_space=pltpu.SMEM)],
        out_specs=vmem,
        scratch_shapes=[
            pltpu.VMEM((16, FEAT, 2 * HID), BF16),
            pltpu.VMEM((HID, D), BF16),
            pltpu.VMEM((TOK, TOK), BF16),
            pltpu.VMEM((TOK, FEAT), BF16),
            pltpu.VMEM((TOK, FEAT), BF16),
            pltpu.VMEM((2 * CAP, TOK), BF16),
            pltpu.VMEM((STEPS, 8, TOK), F32),
            pltpu.VMEM((8, TOK), F32),
            pltpu.VMEM((STEPS, 2) + unit, BF16),
            pltpu.VMEM((STEPS, 16, 2, 2) + unit, BF16),
            pltpu.VMEM((2, 2 * CAP, 2 * HID), F32),
            pltpu.VMEM((2, 2 * CAP, HID), BF16),
            pltpu.VMEM((STEPS, 2, 4, 4, 2) + unit, BF16),
            pltpu.VMEM((STEPS, 2, 5, 2) + unit, BF16),
            pltpu.VMEM((STEPS, 2, 5, 2, 2) + unit, BF16),
            pltpu.VMEM((STEPS, 2, 5, 2) + unit, BF16),
            pltpu.VMEM((STEPS, 2, 4, 2) + unit, BF16),
            pltpu.VMEM((STEPS, 2, 2) + unit, BF16),
            pltpu.VMEM((STEPS, 2, 2) + unit, BF16),
            pltpu.VMEM((STEPS, 2) + tile, F32),
            pltpu.VMEM((STEPS, 3) + tile, F32),
            pltpu.VMEM((STEPS, 3) + tile, F32),
            pltpu.VMEM((STEPS, 2) + tile, F32),
            pltpu.VMEM((STEPS, 2, 2) + tile, F32),
            dma((3,)),
            dma((STEPS, 16, 2, 2)),
            dma((STEPS,)),
            dma((STEPS, 2, 5, 6)),
            dma((STEPS,)),
            dma((STEPS,)),
            dma((STEPS, 6)),
            dma((STEPS, 6)),
            dma((STEPS, 2, 2)),
            dma((STEPS,)),
            dma((STEPS, 2, 2)),
            dma((STEPS,)),
            dma((2,)),
            dma((2,)),
        ],
        compiler_params=pltpu.CompilerParams(
            collective_id=0, has_side_effects=True, vmem_limit_bytes=60 * 1024 * 1024
        ),
        name="moe_relay",
    )(
        tokens,
        norm_gain,
        jnp.transpose(router, (0, 2, 1)),
        w_gate.reshape(16, FEAT, HID),
        w_up.reshape(16, FEAT, HID),
        w_down.reshape(HID, D),
        jnp.transpose(expert_ids, (0, 2, 1)),
        lengths,
    )


def solution(mesh):
    in_specs = (
        P(("section", "expert"), "tensor"),
        P(None, "tensor"),
        P(None, "tensor", None),
        P("section", "expert", None, "tensor"),
        P("section", "expert", None, "tensor"),
        P("section", "expert", "tensor", None),
        P(None, ("section", "expert"), None),
        P(None, "expert"),
    )
    out_specs = P(("section", "expert"), "tensor")
    return jax.shard_map(
        on_device, mesh=mesh, in_specs=in_specs, out_specs=out_specs, check_vma=False
    )
```

time: 603 us -> 121 us (0.20)
  waiting for transfers between devices: 280 us -> 0 us
  blocking collectives: 173 us -> 0 us
  Pallas kernels: 0 us -> 118 us
  local copies, waits for them, and re-layouts: 65.9 us -> 3.13 us
  matrix products: 33.2 us -> 0 us
  other arithmetic: 24.3 us -> 0 us
  between operations: 13.3 us -> 0.01 us
  starting transfers between devices: 11 us -> 0 us
    unnamed x6 -> x0, waiting for transfers between devices: 154 us -> none
    psum x2 -> x0, blocking collectives: 119 us -> none  [moe_layer(): lax.psum((jnp.sum(as_float * as_float, axis=1), part_logits), 'tensor')]
    pallas_call x0 -> x1, Pallas kernels: none -> 118 us  [on_device(): pl.pallas_call(kernel, out_shape=jax.ShapeDtypeStruct((TOK, FEAT), BF16),...]
    all_gather x2 -> x0, waiting for transfers between devices: 106 us -> none  [moe_layer(): feature_piece = lax.all_gather(held_rows, 'tensor', axis=2, tiled=True)]
    all_to_all x4 -> x0, blocking collectives: 53.9 us -> none  [the longest x2 36.8 us: moe_layer(): lax.all_to_all(widened.reshape(expert_count, CAP, feature_count), 'expert...]
    unnamed x39 -> x2, local copies, waits for them, and re-layouts: 56.4 us -> 3.13 us
    dot_general x10 -> x0, matrix products: 33.2 us -> none  [the longest x2 16 us: moe_layer(): jnp.einsum('snf,sfd->snd', hidden, down_w, preferred_element_type=jnp.flo...]
    ppermute x5 -> x0, waiting for transfers between devices: 20.1 us -> none  [the longest x1 14.5 us: from_behind(): return lax.ppermute(x, axis, [(i, (i + by) % peers) for i in range(peers)])]
  transfers between devices with their start and end apart: 9 -> 0, of which waited for: 8 -> 0; matrix products, arithmetic and copies ran while one was open for 2% -> 0% of each run, Pallas kernels for 0% -> 0%
where the time goes in v1:
time: 121 us
  Pallas kernels  118 us (98%)
  local copies, waits for them, and re-layouts  3.13 us (3%)
    pallas_call x1, Pallas kernels, on_device(): pl.pallas_call(kernel, out_shape=jax.ShapeDtypeStruct((TOK, FEAT), BF16),...  118 us
    unnamed x2, local copies, waits for them, and re-layouts  3.13 us

profile of v1, /device:TPU:1, one launch (start us, length us, event | category | flops | bytes accessed | tf_op | source)
XLA Modules:
  0.0 121.2 jit_solution(7998974969821101155)
XLA Ops:
  0.0 1.3 %copy.9.lens_ref = s32[8,4]{1,0:T(8,128)} copy(s32[8,4]{0,1:T(4,128)} %param.15) | data formatting | bytes 256 | tf_op args[7]
  1.3 118.1 %moe_relay.1 = bf16[512,384]{1,0:T(8,128)(2,1)} custom-call(bf16[512,384]{1,0:T(8,128)(2,1)} %x_ref.1, f32[4,384]{1,0:T(4,128)} %gain_ref.1, f32[4,8,384]{2,1,0:T(8,128)} %bitcast.8, bf16[16,384,256]{2,1,0:T(8,128)(2,1)} %bitcast.5, bf16[16,384,256]{2,1,0:T(8,128)(2,1)} %bitcast.6, bf16[256,6144]{1,0:T(8,128)(2,1)} %bitcast.7, s32[2,2,512]{2,1,0:T(2,128)} %bitcast.9, ...), custom_call_target="tpu_custom_call" | custom-call | tf_op jit(solution)/shard_map/moe_relay/pallas_call | solution.py:468
  119.4 1.8 %copy.11 = bf16[512,384]{1,0:T(8,128)(2,1)} copy(bf16[512,384]{1,0:T(8,128)(2,1)} %moe_relay.1) | data formatting | bytes 786432

commit v2 on v1

--- a/solution.py
+++ b/solution.py
@@ -32,7 +32,7 @@
 
 def kernel(
     x_ref, gain_ref, router_ref, gate_hbm, up_hbm, down_hbm, ids_ref, lens_ref, out_ref,
-    w_in, w_down, tri, xc, xn, one_hot, slots, slots_in, rows_out,
+    w_in, w_down, tri, xc, xn, one_hot, choice, taken, slots, slots_in, rows_out,
     ag, acc, hid, pb, passed, landed, mixed, ring, final, back,
     stat, stat_x, stat_y, scales, scales_in,
     w_sem, ag_sem, ag_send, rs_sem, rs_send, ex_send, stat_sem, stat_send,
@@ -77,24 +77,27 @@
     for peer in peers:
         pl.semaphore_signal(barrier, inc=1, device_id=peer, device_id_type=MESH)
 
-    xc[...] = x_ref[...]
-    tri[...] = (
-        lax.broadcasted_iota(jnp.int32, (TOK, TOK), 0) < lax.broadcasted_iota(jnp.int32, (TOK, TOK), 1)
-    ).astype(F32).astype(BF16)
-    pl.semaphore_wait(barrier, len(peers))
-
     def remote(src, dst, send, recv, dev):
         return pltpu.make_async_remote_copy(
             src_ref=src, dst_ref=dst, send_sem=send, recv_sem=recv, device_id=dev, device_id_type=MESH
         )
 
-    def step(st, carry):
+    sub = lax.broadcasted_iota(jnp.int32, (8, 2 * CAP), 0)
+    half = lax.broadcasted_iota(jnp.int32, (8, 2 * CAP), 1) // CAP
+    gain = gain_ref[pl.ds(layer, 1), :]
+
+    def table_of(slot):
+        spot = lax.broadcasted_iota(jnp.int32, (CAP, TOK), 0).astype(F32)
+        parts = [(slot[e : e + 1, :] == spot).astype(F32).astype(BF16) for e in range(2)]
+        return jnp.concatenate(parts, axis=0)
+
+    def route(st):
         first = ids_ref[st, pl.ds(0, 1), :]
         second = ids_ref[st, pl.ds(1, 1), :]
         batch = (sec + 8 - 2 * st) % N_SEC
         lane = lax.broadcasted_iota(jnp.int32, (1, SEQ_LEN), 1)
         live = jnp.concatenate(
-            [(lane < lens_ref[batch, q]).astype(jnp.int32) for q in range(TOK // SEQ_LEN)], axis=1
+            [(lane < lens_ref[q, batch]).astype(jnp.int32) for q in range(TOK // SEQ_LEN)], axis=1
         )
         row_id = lax.broadcasted_iota(jnp.int32, (8, TOK), 0)
         named = (
@@ -105,29 +108,8 @@
         earlier = jnp.dot(named.astype(BF16), tri[...], preferred_element_type=F32)
         slot = jnp.where((named > 0.5) & (earlier < CAP - 0.5), earlier, -1.0)
         slots[st] = slot
-        spot = lax.broadcasted_iota(jnp.int32, (CAP, TOK), 0).astype(F32)
-        for e in range(2):
-            one_hot[pl.ds(e * CAP, CAP), :] = (slot[e : e + 1, :] == spot).astype(F32).astype(BF16)
-        picks = one_hot[...]
-        rows = jnp.dot(picks, xc[...], preferred_element_type=F32)
-        scaled = rows * gain_ref[pl.ds(layer, 1), :]
-        rows_out[st] = scaled.astype(BF16).reshape(2, CAP, FEAT)
-
-        pltpu.make_async_copy(rows_out.at[st, core], ag.at[st, t, core, 0], ag_sem.at[st, t, core, 0]).start()
-        remote(
-            rows_out.at[st, other], ag.at[st, t, core, 0], ex_send.at[st], ag_sem.at[st, t, core, 0],
-            (sec, other, t),
-        ).start()
-        for e in range(2):
-            remote(
-                rows_out.at[st, e], ag.at[st, t, core, 1], ex_send.at[st], ag_sem.at[st, t, core, 1],
-                (mate, e, t),
-            ).start()
-
-        sub = lax.broadcasted_iota(jnp.int32, (8, 2 * CAP), 0)
-        half = lax.broadcasted_iota(jnp.int32, (8, 2 * CAP), 1) // CAP
-        squares = lax.dot_general(jnp.ones((8, FEAT), F32), rows * rows, NT, precision=HIGHEST, preferred_element_type=F32)
-        logits = lax.dot_general(router_ref[layer], scaled, NT, precision=HIGHEST, preferred_element_type=F32)
+        picks = table_of(slot)
+        one_hot[st] = picks
         chosen = []
         for e in range(2):
             rest = jnp.where(first == e, second, first)
@@ -136,9 +118,49 @@
                     (rest == row_id).astype(F32).astype(BF16), picks, NT, preferred_element_type=F32
                 )
             )
-        rival = jnp.where(half == 0, chosen[0], chosen[1])
-        gap = jnp.sum(logits * ((sub == half).astype(F32) - rival), axis=0, keepdims=True)
+        choice[st] = (sub == half).astype(F32) - jnp.where(half == 0, chosen[0], chosen[1])
+
+    def take_rows(st, value):
+        rows = jnp.dot(one_hot[st], value, preferred_element_type=F32)
+        taken[...] = rows
+        rows_out[st] = (rows * gain).astype(BF16).reshape(2, CAP, FEAT)
+
+    def measure_rows(st):
+        rows = taken[...]
+        squares = lax.dot_general(jnp.ones((8, FEAT), F32), rows * rows, NT, precision=HIGHEST, preferred_element_type=F32)
+        logits = lax.dot_general(router_ref[layer], rows * gain, NT, precision=HIGHEST, preferred_element_type=F32)
+        gap = jnp.sum(logits * choice[st], axis=0, keepdims=True)
         stat[st, 0] = jnp.where(sub == 0, squares, jnp.where(sub == 1, gap, 0.0))
+
+    tri[...] = (
+        lax.broadcasted_iota(jnp.int32, (TOK, TOK), 0) < lax.broadcasted_iota(jnp.int32, (TOK, TOK), 1)
+    ).astype(F32).astype(BF16)
+    route(0)
+    take_rows(0, x_ref[...])
+    measure_rows(0)
+    pl.semaphore_wait(barrier, len(peers))
+
+    def step(st, carry):
+        remote(
+            rows_out.at[st, other], ag.at[st, t, core, 0], ex_send.at[st], ag_sem.at[st, t, core, 0],
+            (sec, other, t),
+        ).start()
+        for e in range(2):
+            remote(
+                rows_out.at[st, e], ag.at[st, t, core, 1], ex_send.at[st], ag_sem.at[st, t, core, 1],
+                (mate, e, t),
+            ).start()
+        for off in ((1, 0), (-1, 0), (0, 1), (0, -1)):
+            remote(
+                rows_out.at[st, core], ag.at[st, t, core, 0], ag_send.at[st], ag_sem.at[st, t, core, 0],
+                (sec, core, at(*off)),
+            ).start()
+        pltpu.make_async_copy(rows_out.at[st, core], ag.at[st, t, core, 0], ag_sem.at[st, t, core, 0]).start()
+
+        @pl.when(st == 1)
+        def _():
+            measure_rows(1)
+
         for d in (1, 2, 3):
             remote(
                 stat.at[st, 0], stat_x.at[st, d - 1], stat_send.at[st, d - 1], stat_sem.at[st, d - 1],
@@ -148,7 +170,6 @@
         @pl.when(st == 0)
         def _():
             remote(slots.at[0], slots_in, tok_send.at[0], tok_sem.at[0], (ahead, core, t)).start()
-            remote(x_ref, xn, tok_send.at[1], tok_sem.at[1], (ahead, core, t)).start()
 
         def unit_send(s, sg, which, role, d):
             remote(
@@ -166,16 +187,15 @@
             for d in (1, -1):
                 unit_send(s, sg, which, 1, d)
 
-        def own(sg):
-            for s in range(2):
-                unit_wait(s, sg, t)
-            for s in range(2):
-                for d in (1, -1):
-                    unit_send(s, sg, t, 0, d)
-            for s in range(2):
-                across(s, sg, t)
-
-        own(0)
+        def own(s, sg):
+            unit_wait(s, sg, t)
+            for off in ((1, 0), (-1, 0), (0, 1), (0, -1)):
+                remote(
+                    ag.at[st, t, s, sg], ag.at[st, t, s, sg], ag_send.at[st], ag_sem.at[st, t, s, sg],
+                    (sec, core, at(*off)),
+                ).start()
+
+        own(other, 0)
         total = stat[st, 0]
         for d in (1, 2, 3):
             remote(
@@ -189,7 +209,8 @@
                 stat.at[st, 1], stat_y.at[st, d - 1], stat_send.at[st, d + 2], stat_sem.at[st, d + 2],
                 (sec, core, at(0, d)),
             ).start()
-        own(1)
+        own(0, 1)
+        own(1, 1)
         for s in range(2):
             left, right = shard(s, -1, 0), shard(s, 1, 0)
             unit_wait(s, 0, left)
@@ -232,9 +253,11 @@
                 across(s, sg, far)
 
         acc[...] = jnp.zeros_like(acc)
+        unit_wait(core, 0, t)
 
         @pl.when(st == 0)
         def _():
+            route(1)
             w_copies[0].wait()
             w_copies[1].wait()
 
@@ -291,6 +314,7 @@
 
         @pl.when(st == 0)
         def _():
+            remote(x_ref, xn, tok_send.at[1], tok_sem.at[1], (ahead, core, t)).start()
             w_copies[2].wait()
 
         def ring_send(s, k, m, src, dst, role, d):
@@ -406,13 +430,11 @@
                     ).start()
             remote(slots.at[0], slots_in, tok_send.at[0], tok_sem.at[0], (ahead, core, t)).wait_recv()
             remote(x_ref, xn, tok_send.at[1], tok_sem.at[1], (ahead, core, t)).wait_recv()
-            for e in range(2):
-                one_hot[pl.ds(e * CAP, CAP), :] = (
-                    slots_in[e : e + 1, :] == spot
-                ).astype(F32).astype(BF16)
-            table = one_hot[...]
+            table = table_of(slots_in[...])
             back_wait()
-            xc[...] = combined(xn[...], table)
+            value = combined(xn[...], table)
+            xc[...] = value
+            take_rows(1, value)
 
         @pl.when(st == 1)
         def _():
@@ -427,7 +449,7 @@
                     (mate, s, t),
                 ).start()
             back_wait()
-            out_ref[...] = combined(xc[...], one_hot[...])
+            out_ref[...] = combined(xc[...], one_hot[1])
 
         sixty = ag.at[st, pl.ds(0, 15)]
         remote(sixty, sixty, ag_send.at[st], ag_sem.at[st, 0, 0, 0], (sec, other, t)).wait_send()
@@ -476,7 +498,9 @@
             pltpu.VMEM((TOK, TOK), BF16),
             pltpu.VMEM((TOK, FEAT), BF16),
             pltpu.VMEM((TOK, FEAT), BF16),
-            pltpu.VMEM((2 * CAP, TOK), BF16),
+            pltpu.VMEM((STEPS, 2 * CAP, TOK), BF16),
+            pltpu.VMEM((STEPS,) + tile, F32),
+            pltpu.VMEM((2 * CAP, FEAT), F32),
             pltpu.VMEM((STEPS, 8, TOK), F32),
             pltpu.VMEM((8, TOK), F32),
             pltpu.VMEM((STEPS, 2) + unit, BF16),
@@ -522,7 +546,7 @@
         w_up.reshape(16, FEAT, HID),
         w_down.reshape(HID, D),
         jnp.transpose(expert_ids, (0, 2, 1)),
-        lengths,
+        jnp.transpose(lengths),
     )
 
 

time: 121 us -> 114 us (0.942)
  Pallas kernels: 118 us -> 112 us
  local copies, waits for them, and re-layouts: 3.13 us -> 1.78 us
    pallas_call x1, Pallas kernels: 118 us -> 112 us  [on_device(): pl.pallas_call(kernel, out_shape=jax.ShapeDtypeStruct((TOK, FEAT), BF16),...]
    unnamed x2 -> x1, local copies, waits for them, and re-layouts: 3.13 us -> 1.78 us
where the time goes in v2:
time: 114 us
  Pallas kernels  112 us (98%)
  local copies, waits for them, and re-layouts  1.78 us (2%)
    pallas_call x1, Pallas kernels, on_device(): pl.pallas_call(kernel, out_shape=jax.ShapeDtypeStruct((TOK, FEAT), BF16),...  112 us

profile of v2, /device:TPU:1, one launch (start us, length us, event | category | flops | bytes accessed | tf_op | source)
XLA Modules:
  0.0 113.7 jit_solution(2968717047346699188)
XLA Ops:
  0.0 111.9 %moe_relay.1 = bf16[512,384]{1,0:T(8,128)(2,1)} custom-call(bf16[512,384]{1,0:T(8,128)(2,1)} %x_ref.1, f32[4,384]{1,0:T(4,128)} %gain_ref.1, f32[4,8,384]{2,1,0:T(8,128)} %bitcast.9, bf16[16,384,256]{2,1,0:T(8,128)(2,1)} %bitcast.6, bf16[16,384,256]{2,1,0:T(8,128)(2,1)} %bitcast.7, bf16[256,6144]{1,0:T(8,128)(2,1)} %bitcast.8, s32[2,2,512]{2,1,0:T(2,128)} %bitcast.10, ...), custom_call_target="tpu_custom_call" | custom-call | tf_op jit(solution)/shard_map/moe_relay/pallas_call | solution.py:490
  111.9 1.8 %copy.10 = bf16[512,384]{1,0:T(8,128)(2,1)} copy(bf16[512,384]{1,0:T(8,128)(2,1)} %moe_relay.1) | data formatting | bytes 786432
